TPU v7x, 32 devices: a whole 2x2x4 slice. The times are simulated.
32 devices in a mesh: prow: 8 (over z, core), pcol: 4 (over y, x).
Axes of the slice: x: 2, y: 2, z: 4, core: 2. Of those that a mesh axis runs over, the one named last changes fastest.
Arguments:
- right_side: float32 [1024, 4, 4, 1024], P('prow', None, 'pcol'), may hold values from -6 to 6
- inverse_blocks: bfloat16 [2, 1, 8, 1024, 2, 4, 1024], P(None, None, 'prow', None, None, 'pcol'), as said below
- coupling: bfloat16 [1, 8, 1024, 2, 4, 1024], P(None, 'prow', None, None, 'pcol'), may hold values from -0.03125 to 0.03125
- pivots: int32 [2, 8, 1024], P(None, 'prow'), may hold values from 0 to 16383, as said below
Outputs:
- solution: bfloat16 [1024, 2, 8, 1024], P('pcol', None, 'prow')
Inputs may be any that keep to these rules, and one draw needn't show every extreme that they name: `inverse_blocks`: each block is unit upper triangular: ones on its diagonal, zeros below it. Every row number of the window appears exactly once; for every p and p2, exactly 16 * 1024 / 8 ** 2 of the entries pivots[:, p, :] are rows g with (g // 1024) % 8 == p2.
All inputs are finite; a program needn't handle non-finite values.
Results may differ from a plain program's by a relative error of at most 0.0052.
Values may be sent and summed in bfloat16 or wider, within the bound.
A program may use at most 128 MiB of HBM per device.

v0:
```python
import jax
import jax.numpy as jnp
from jax import lax
from jax.sharding import PartitionSpec as P


def body(right_side, inverse_blocks, coupling, pivots):
    rhs_here = right_side.shape[0]
    tiles_across = right_side.shape[1]
    tile_width = right_side.shape[3]
    count_rows = inverse_blocks.shape[1] * tile_width
    count_cols = inverse_blocks.shape[4] * tile_width
    blocks_here = inverse_blocks.shape[1]
    inverse_pair = inverse_blocks.reshape(2, count_rows, count_cols)
    coupling_mat = coupling.reshape(count_rows, count_cols)
    flat_rhs = right_side.reshape(rhs_here, tiles_across * tile_width)
    lower_rhs = flat_rhs[:, :count_cols]
    upper_rhs = flat_rhs[:, count_cols:]
    row_devices = lax.axis_size("prow")
    rhs_total = rhs_here * row_devices
    own_cols = rhs_total // lax.axis_size("pcol")
    contract_last = (((1,), (1,)), ((), ()))

    def solve_with(inverse_mat, portion):
        return lax.dot_general(
            portion, inverse_mat, contract_last, preferred_element_type=jnp.float32
        )

    def as_tiles(solved):
        return solved.reshape(own_cols, blocks_here, 1, tile_width)

    first_partial = solve_with(
        inverse_pair[1], lax.all_gather(upper_rhs.astype(jnp.bfloat16), "prow", axis=0, tiled=True)
    )
    upper_solved = lax.psum_scatter(first_partial, "pcol", scatter_dimension=0, tiled=True).astype(
        jnp.bfloat16
    )
    update_partial = jnp.dot(
        lax.all_gather(upper_solved, "pcol", axis=0, tiled=True),
        coupling_mat,
        preferred_element_type=jnp.float32,
    )
    update = lax.psum_scatter(update_partial, "prow", scatter_dimension=0, tiled=True)
    lower_ready = (lower_rhs - update).astype(jnp.bfloat16)
    second_partial = solve_with(
        inverse_pair[0], lax.all_gather(lower_ready, "prow", axis=0, tiled=True)
    )
    lower_solved = lax.psum_scatter(second_partial, "pcol", scatter_dimension=0, tiled=True).astype(
        jnp.bfloat16
    )
    joined = jnp.concatenate([as_tiles(lower_solved), as_tiles(upper_solved)], axis=1)
    all_rows = lax.all_gather(joined, "prow", axis=2, tiled=True).reshape(own_cols, -1)
    permuted = jnp.take(all_rows, pivots.reshape(-1), axis=1)
    return permuted.reshape(own_cols, pivots.shape[0], 1, tile_width)


def solution(mesh):
    in_specs = (
        P("prow", None, "pcol", None),
        P(None, None, "prow", None, None, "pcol", None),
        P(None, "prow", None, None, "pcol", None),
        P(None, "prow", None),
    )
    out_specs = P("pcol", None, "prow", None)
    return jax.shard_map(body, mesh=mesh, in_specs=in_specs, out_specs=out_specs, check_vma=False)
```

profile of v0, /device:TPU:0, one launch (start us, length us, event | category | flops | bytes accessed | tf_op | source)
XLA Modules:
  0.0 492.8 jit_solution(14746014707884761754)
XLA Ops:
  6.5 0.0 all-gather.5.cloned.1.call-start
  6.5 7.1 %reduce = f32[128,4,1024]{2,1,0:T(4,128)S(1)} reduce(f32[128,4,1,1024]{3,2,1,0:T(1,128)} %param.4, f32[]{:T(128)} %constant.20), dimensions={2}, to_apply=%param.4.reduce_sub_computation | reduce | bytes 4194308 | tf_op args[0]
  13.6 1.6 copy.9
  15.3 0.0 copy-start
  15.3 1.3 copy-done
  16.6 0.9 slice.27
  17.5 0.0 all-gather.5.cloned.1.call-update
  17.5 0.2 reduce-scatter.4.cloned.1.call-start
  17.7 7.9 %fusion.1 = (bf16[1,1,1,1024,2,1,1024]{6,4,5,3,2,1,0:T(2,128)(2,1)}, bf16[1,1,1,1024,2,1,1024]{6,4,5,3,2,1,0:T(2,128)(2,1)S(1)}) fusion(bf16[2,1,1,1024,2,1,1024]{6,4,5,3,2,1,0:T(2,128)(2,1)} %param.5), kind=kLoop, calls=%fused_computation.11 | loop fusion | bytes 16777216 | tf_op jit(solution)/shard_map/slice | solution.py:46
  25.7 3.3 copy.10
  29.0 38.2 %all-gather.5.cloned.1.call-done = bf16[1024,2048]{1,0:T(8,128)(2,1)} async-done(((bf16[128,2048]{1,0:T(8,128)(2,1)}), bf16[1024,2048]{1,0:T(8,128)(2,1)}) %all-gather.5.cloned.1.call-update) | async-done | bytes 4194320 | tf_op jit(solution)/shard_map/all_gather | solution.py:33
  67.2 10.0 %fusion.2 = f32[1024,1024]{1,0:T(8,128)} fusion(bf16[1024,2048]{1,0:T(8,128)(2,1)} %all-gather.5.cloned.1.call-done, bf16[1024,2048]{1,0:T(8,128)(2,1)} %bitcast.39), kind=kOutput, calls=%fused_computation.12 | convolution fusion | flops 4294967296 | bytes 12582912 | tf_op jit(solution)/shard_map/dot_general | solution.py:25
  77.2 0.0 reduce-scatter.4.cloned.1.call-update
  77.2 0.0 all-gather.7.cloned.1.call-start
  77.3 51.5 %reduce-scatter.4.cloned.1.call-done = f32[256,1024]{1,0:T(8,128)} async-done(((f32[1024,1024]{1,0:T(8,128)}), f32[256,1024]{1,0:T(8,128)}) %reduce-scatter.4.cloned.1.call-update) | async-done | bytes 1048592 | tf_op jit(solution)/shard_map/reduce_scatter | solution.py:35
  128.8 2.1 convert_element_type.10
  130.9 0.0 all-gather.7.cloned.1.call-update
  130.9 0.0 reduce-scatter.6.cloned.1.call-start
  131.0 5.5 %copy.11 = bf16[128,8,2,1024]{3,1,2,0:T(8,128)(2,1)} copy(bf16[128,8,2,1024]{3,2,1,0:T(2,128)(2,1)} %bitcast.38) | data formatting | bytes 8388608
  136.5 29.7 %all-gather.7.cloned.1.call-done = bf16[1024,1024]{1,0:T(8,128)(2,1)} async-done(((bf16[256,1024]{1,0:T(8,128)(2,1)}), bf16[1024,1024]{1,0:T(8,128)(2,1)}) %all-gather.7.cloned.1.call-update) | async-done | bytes 2097168 | tf_op jit(solution)/shard_map/all_gather | solution.py:39
  166.3 10.5 %fusion.3 = f32[1024,2048]{1,0:T(8,128)} fusion(bf16[1024,1024]{1,0:T(8,128)(2,1)} %all-gather.7.cloned.1.call-done, bf16[1024,2048]{1,0:T(8,128)(2,1)} %bitcast.41), kind=kOutput, calls=%fused_computation.13 | convolution fusion | flops 4294967296 | bytes 14680064 | tf_op jit(solution)/shard_map/dot_general | solution.py:38
  176.8 0.0 copy-start.1
  176.8 0.0 reduce-scatter.6.cloned.1.call-update
  176.8 0.0 all-gather.9.cloned.1.call-start
  176.9 89.6 %reduce-scatter.6.cloned.1.call-done = f32[128,2048]{1,0:T(8,128)} async-done(((f32[1024,2048]{1,0:T(8,128)}), f32[128,2048]{1,0:T(8,128)}) %reduce-scatter.6.cloned.1.call-update) | async-done | bytes 1048592 | tf_op jit(solution)/shard_map/reduce_scatter | solution.py:43
  266.5 0.0 copy-done.1
  266.5 2.1 fusion
  268.6 0.0 all-gather.9.cloned.1.call-update
  268.7 0.3 reduce-scatter.8.cloned.1.call-start
  268.9 5.5 %copy.12 = bf16[128,8,2,1024]{3,1,2,0:T(8,128)(2,1)} copy(bf16[128,8,2,1024]{3,2,1,0:T(2,128)(2,1)} %bitcast.33) | data formatting | bytes 8388608
  274.5 39.7 %all-gather.9.cloned.1.call-done = bf16[1024,2048]{1,0:T(8,128)(2,1)} async-done(((bf16[128,2048]{1,0:T(8,128)(2,1)}), bf16[1024,2048]{1,0:T(8,128)(2,1)}) %all-gather.9.cloned.1.call-update) | async-done | bytes 4194320 | tf_op jit(solution)/shard_map/all_gather | solution.py:46
  314.1 9.9 %fusion.4 = f32[1024,1024]{1,0:T(8,128)} fusion(bf16[1024,2048]{1,0:T(8,128)(2,1)} %all-gather.9.cloned.1.call-done, bf16[1024,2048]{1,0:T(8,128)(2,1)} %bitcast.40), kind=kOutput, calls=%fused_computation.14 | convolution fusion | flops 4294967296 | bytes 12582912 | tf_op jit(solution)/shard_map/dot_general | solution.py:25
  324.1 0.0 copy-start.2
  324.1 0.0 reduce-scatter.8.cloned.1.call-update
  324.1 0.0 copy-start.3
  324.1 0.0 all-gather.11.cloned.1.call-start
  324.2 1.1 copy-done.2
  325.3 0.1 convert_bitcast_fusion.1
  325.4 50.3 %reduce-scatter.8.cloned.1.call-done = f32[256,1024]{1,0:T(8,128)} async-done(((f32[1024,1024]{1,0:T(8,128)}), f32[256,1024]{1,0:T(8,128)}) %reduce-scatter.8.cloned.1.call-update) | async-done | bytes 1048592 | tf_op jit(solution)/shard_map/reduce_scatter | solution.py:48
  375.7 1.3 convert_bitcast_fusion
  377.0 1.1 pad_maximum_fusion
  378.0 0.0 all-gather.11.cloned.1.call-update
  378.0 0.0 copy-done.3
  378.1 82.1 %all-gather.11.cloned.1.call-done = bf16[256,2,8,1024]{3,0,2,1:T(8,128)(2,1)} async-done(((bf16[256,2,1,1024]{3,0,2,1:T(8,128)(2,1)}), bf16[256,2,8,1024]{3,0,2,1:T(8,128)(2,1)}) %all-gather.11.cloned.1.call-update) | async-done | bytes 8388624 | tf_op jit(solution)/shard_map/all_gather | solution.py:52
  460.2 11.6 %copy.6 = bf16[256,2,8,1024]{0,3,2,1:T(8,128)(2,1)} copy(bf16[256,2,8,1024]{3,0,2,1:T(8,128)(2,1)} %all-gather.11.cloned.1.call-done) | data formatting | bytes 16777216 | tf_op jit(solution)/shard_map/all_gather | solution.py:52
  471.8 11.1 %gather_fusion = bf16[2048,256]{1,0:T(8,128)(2,1)S(1)} fusion(bf16[256,16384]{0,1:T(8,128)(2,1)} %bitcast.32, s32[2048]{0:T(1024)S(1)} %broadcast_clamp_fusion), kind=kCustom, calls=%fused_computation | custom fusion | bytes 2105344 | tf_op jit(solution)/shard_map/jit(_take)/gather | solution.py:53
  482.9 1.1 copy.7
  484.1 1.9 broadcast_select_fusion
  (3 shorter events, 0.0 us)
Async XLA Ops:
  6.5 60.7 %all-gather.5.cloned.1.call-start = ((), (), s32[]{:S(2)}) async-start(), calls=%async_computation.3 | async-start | bytes 4718592 | tf_op jit(solution)/shard_map/all_gather | solution.py:33
  15.3 1.3 copy-start
  17.5 111.3 %reduce-scatter.4.cloned.1.call-start = ((), (), s32[]{:S(2)}) async-start(), calls=%async_computation.4 | async-start | bytes 5242880 | tf_op jit(solution)/shard_map/reduce_scatter | solution.py:35
  77.2 89.0 %all-gather.7.cloned.1.call-start = ((), (), s32[]{:S(2)}) async-start(), calls=%async_computation.5 | async-start | bytes 2621440 | tf_op jit(solution)/shard_map/all_gather | solution.py:39
  130.9 135.6 %reduce-scatter.6.cloned.1.call-start = ((), (), s32[]{:S(2)}) async-start(), calls=%async_computation.6 | async-start | bytes 9437184 | tf_op jit(solution)/shard_map/reduce_scatter | solution.py:43
  176.8 89.7 %copy-start.1 = (f32[16,8,4,1024]{3,1,2,0:T(8,128)S(1)}, f32[16,8,4,1024]{3,1,2,0:T(8,128)}, u32[]{:S(2)}) copy-start(f32[16,8,4,1024]{3,1,2,0:T(8,128)} %copy-done) | copy-start | bytes 6291460
  176.8 137.3 %all-gather.9.cloned.1.call-start = ((), (), s32[]{:S(2)}) async-start(), calls=%async_computation.7 | async-start | bytes 4718592 | tf_op jit(solution)/shard_map/all_gather | solution.py:46
  268.7 107.0 %reduce-scatter.8.cloned.1.call-start = ((), (), s32[]{:S(2)}) async-start(), calls=%async_computation.8 | async-start | bytes 5242880 | tf_op jit(solution)/shard_map/reduce_scatter | solution.py:48
  324.1 1.2 copy-start.2
  324.1 53.9 %copy-start.3 = (s32[2,1,1024]{2,1,0:T(1,128)S(1)}, s32[2,1,1024]{2,1,0:T(1,128)}, u32[]{:S(2)}) copy-start(s32[2,1,1024]{2,1,0:T(1,128)} %param.7) | copy-start | bytes 24580
  324.1 136.1 %all-gather.11.cloned.1.call-start = ((), (), s32[]{:S(2)}) async-start(), calls=%async_computation.9 | async-start | bytes 9437184 | tf_op jit(solution)/shard_map/all_gather | solution.py:52
Sparse Core Ops, SparseCore 0:
  17.6 49.5 all-gather.4
  77.4 51.3 reduce-scatter.3
  131.0 35.1 all-gather.6
  176.9 89.5 reduce-scatter.5
  268.8 45.3 all-gather.8
  324.2 51.3 reduce-scatter.7
  378.2 82.0 all-gather.10
where the time goes:
time: 494 us; the launch traced here: 493 us
  waiting for transfers between devices  381 us (77%)
  local copies, waits for them, and re-layouts  51.2 us (10%)
  matrix products  30.4 us (6%)
  other arithmetic  15.6 us (3%)
  between operations  13.6 us (3%)
    reduce_scatter x1, waiting for transfers between devices, body(): lax.psum_scatter(update_partial, 'prow', scatter_dimension=0, tiled=True)  89.6 us
    all_gather x1, waiting for transfers between devices, body(): lax.all_gather(joined, 'prow', axis=2, tiled=True).reshape(own_cols, -1)  82.1 us
    reduce_scatter x1, waiting for transfers between devices, body(): lax.psum_scatter(first_partial, 'pcol', scatter_dimension=0, tiled=True)  51.5 us
    reduce_scatter x1, waiting for transfers between devices, body(): lax.psum_scatter(second_partial, 'pcol', scatter_dimension=0, tiled=True)  50.3 us
    all_gather x1, waiting for transfers between devices, body(): lax.all_gather(lower_ready, 'prow', axis=0, tiled=True)  39.7 us
    all_gather x1, waiting for transfers between devices, body(): lax.all_gather(upper_rhs.astype(jnp.bfloat16), 'prow', axis=0, tiled=True)  38.2 us
    all_gather x1, waiting for transfers between devices, body(): lax.all_gather(upper_solved, 'pcol', axis=0, tiled=True)  29.7 us
    dot_general x2, matrix products, solve_with(): lax.dot_general(portion, inverse_mat, contract_last, preferred_element_ty...  19.9 us
  transfers between devices with their start and end apart: 7, of which 7 were waited for; matrix products, arithmetic and copies ran while one was open for 5% of the time, Pallas kernels for 0%

commit v1 on v0

--- a/solution.py
+++ b/solution.py
@@ -2,6 +2,28 @@
 import jax.numpy as jnp
 from jax import lax
 from jax.sharding import PartitionSpec as P
+
+
+def joined_along(tiles, dim):
+    tiles = jnp.moveaxis(tiles, 0, dim)
+    lengths = tiles.shape
+    return tiles.reshape(*lengths[:dim], lengths[dim] * lengths[dim + 1], *lengths[dim + 2 :])
+
+
+def gather_around(x, axis, dim):
+    devices = lax.axis_size(axis)
+    pairs = [(i, (i + 1) % devices) for i in range(devices)]
+    back = [(b, a) for a, b in pairs]
+    lower, upper = ([], [])
+    for lap in range(devices - 1):
+        if lap % 2 == 0:
+            lower.append(lax.ppermute(lower[-1] if lower else x, axis, pairs))
+        else:
+            upper.append(lax.ppermute(upper[-1] if upper else x, axis, back))
+    parts = jnp.stack([*lower[::-1], x, *upper])
+    shift = lax.axis_index(axis) - len(lower)
+    parts = parts[(jnp.arange(devices) - shift) % devices]
+    return joined_along(parts, dim)
 
 
 def body(right_side, inverse_blocks, coupling, pivots):
@@ -49,7 +71,7 @@
         jnp.bfloat16
     )
     joined = jnp.concatenate([as_tiles(lower_solved), as_tiles(upper_solved)], axis=1)
-    all_rows = lax.all_gather(joined, "prow", axis=2, tiled=True).reshape(own_cols, -1)
+    all_rows = gather_around(joined, "prow", 2).reshape(own_cols, -1)
     permuted = jnp.take(all_rows, pivots.reshape(-1), axis=1)
     return permuted.reshape(own_cols, pivots.shape[0], 1, tile_width)
 

time: 494 us -> 525 us (1.063)
  local copies, waits for them, and re-layouts: 51.2 us -> 70.6 us
  starting transfers between devices: 0.65 us -> 11.4 us
    ppermute x0 -> x7, waiting for transfers between devices: none -> 82.8 us  [the longest x4 82.8 us: gather_around(): lower.append(lax.ppermute(lower[-1] if lower else x, axis, pairs))]
    all_gather x1 -> x0, waiting for transfers between devices: 82.1 us -> none  [body(): lax.all_gather(joined, 'prow', axis=2, tiled=True).reshape(own_cols, -1)]
    transpose x0 -> x1, local copies, waits for them, and re-layouts: none -> 11.9 us  [joined_along(): tiles = jnp.moveaxis(tiles, 0, dim)]
    all_gather x1 -> x0, local copies, waits for them, and re-layouts: 11.6 us -> none  [body(): lax.all_gather(joined, 'prow', axis=2, tiled=True).reshape(own_cols, -1)]
    ppermute x0 -> x7, starting transfers between devices: none -> 10.7 us  [the longest x3 10.7 us: gather_around(): upper.append(lax.ppermute(upper[-1] if upper else x, axis, back))]
    unnamed x12 -> x18, local copies, waits for them, and re-layouts: 18.6 us -> 28.6 us
    gather x0 -> x1, local copies, waits for them, and re-layouts: none -> 8.07 us  [gather_around(): parts = parts[(jnp.arange(devices) - shift) % devices]]
  transfers between devices with their start and end apart: 7 -> 13, of which waited for: 7 -> 10; matrix products, arithmetic and copies ran while one was open for 5% -> 6% of each run, Pallas kernels for 0% -> 0%
where the time goes in v1:
time: 525 us; the launch traced here: 524 us
  waiting for transfers between devices  382 us (73%)
  local copies, waits for them, and re-layouts  70.6 us (13%)
  matrix products  30.5 us (6%)
  other arithmetic  15.8 us (3%)
  between operations  13.6 us (3%)
  starting transfers between devices  11.4 us (2%)
    reduce_scatter x1, waiting for transfers between devices, body(): lax.psum_scatter(update_partial, 'prow', scatter_dimension=0, tiled=True)  89.6 us
    ppermute x4, waiting for transfers between devices, gather_around(): lower.append(lax.ppermute(lower[-1] if lower else x, axis, pairs))  82.8 us
    reduce_scatter x1, waiting for transfers between devices, body(): lax.psum_scatter(first_partial, 'pcol', scatter_dimension=0, tiled=True)  51.5 us
    reduce_scatter x1, waiting for transfers between devices, body(): lax.psum_scatter(second_partial, 'pcol', scatter_dimension=0, tiled=True)  50.3 us
    all_gather x1, waiting for transfers between devices, body(): lax.all_gather(lower_ready, 'prow', axis=0, tiled=True)  39.7 us
    all_gather x1, waiting for transfers between devices, body(): lax.all_gather(upper_rhs.astype(jnp.bfloat16), 'prow', axis=0, tiled=True)  38.2 us
    all_gather x1, waiting for transfers between devices, body(): lax.all_gather(upper_solved, 'pcol', axis=0, tiled=True)  29.8 us
    unnamed x18, local copies, waits for them, and re-layouts  28.6 us
  transfers between devices with their start and end apart: 13, of which 10 were waited for; matrix products, arithmetic and copies ran while one was open for 6% of the time, Pallas kernels for 0%

profile of v1, /device:TPU:0, one launch (start us, length us, event | category | flops | bytes accessed | tf_op | source)
XLA Modules:
  0.0 523.8 jit_solution(15859851625660539404)
XLA Ops:
  6.5 7.1 %reduce = f32[128,4,1024]{2,1,0:T(4,128)S(1)} reduce(f32[128,4,1,1024]{3,2,1,0:T(1,128)} %param.4, f32[]{:T(128)} %constant.45), dimensions={2}, to_apply=%param.4.reduce_sub_computation | reduce | bytes 4194308 | tf_op args[0]
  13.6 1.6 copy.11
  15.3 1.3 copy-done
  16.6 0.9 slice.29
  17.5 0.2 reduce-scatter.4.cloned.1.call-start
  17.7 7.9 %fusion.4 = (bf16[1,1,1,1024,2,1,1024]{6,4,5,3,2,1,0:T(2,128)(2,1)}, bf16[1,1,1,1024,2,1,1024]{6,4,5,3,2,1,0:T(2,128)(2,1)S(1)}) fusion(bf16[2,1,1,1024,2,1,1024]{6,4,5,3,2,1,0:T(2,128)(2,1)} %param.5), kind=kLoop, calls=%fused_computation.28 | loop fusion | bytes 16777216 | tf_op jit(solution)/shard_map/slice | solution.py:68
  25.7 3.3 copy.12
  29.0 38.2 %all-gather.4.cloned.1.call-done = bf16[1024,2048]{1,0:T(8,128)(2,1)} async-done(((bf16[128,2048]{1,0:T(8,128)(2,1)}), bf16[1024,2048]{1,0:T(8,128)(2,1)}) %all-gather.4.cloned.1.call-update) | async-done | bytes 4194320 | tf_op jit(solution)/shard_map/all_gather | solution.py:55
  67.3 10.0 %fusion.5 = f32[1024,1024]{1,0:T(8,128)} fusion(bf16[1024,2048]{1,0:T(8,128)(2,1)} %all-gather.4.cloned.1.call-done, bf16[1024,2048]{1,0:T(8,128)(2,1)} %bitcast.64), kind=kOutput, calls=%fused_computation.29 | convolution fusion | flops 4294967296 | bytes 12582912 | tf_op jit(solution)/shard_map/dot_general | solution.py:47
  77.2 0.0 all-gather.6.cloned.1.call-start
  77.3 51.5 %reduce-scatter.4.cloned.1.call-done = f32[256,1024]{1,0:T(8,128)} async-done(((f32[1024,1024]{1,0:T(8,128)}), f32[256,1024]{1,0:T(8,128)}) %reduce-scatter.4.cloned.1.call-update) | async-done | bytes 1048592 | tf_op jit(solution)/shard_map/reduce_scatter | solution.py:57
  128.8 2.1 convert_element_type.10
  130.9 0.0 reduce-scatter.6.cloned.1.call-start
  131.0 5.5 %copy.13 = bf16[128,8,2,1024]{3,1,2,0:T(8,128)(2,1)} copy(bf16[128,8,2,1024]{3,2,1,0:T(2,128)(2,1)} %bitcast.63) | data formatting | bytes 8388608
  136.5 29.8 %all-gather.6.cloned.1.call-done = bf16[1024,1024]{1,0:T(8,128)(2,1)} async-done(((bf16[256,1024]{1,0:T(8,128)(2,1)}), bf16[1024,1024]{1,0:T(8,128)(2,1)}) %all-gather.6.cloned.1.call-update) | async-done | bytes 2097168 | tf_op jit(solution)/shard_map/all_gather | solution.py:61
  166.3 10.6 %fusion.6 = f32[1024,2048]{1,0:T(8,128)} fusion(bf16[1024,1024]{1,0:T(8,128)(2,1)} %all-gather.6.cloned.1.call-done, bf16[1024,2048]{1,0:T(8,128)(2,1)} %bitcast.66), kind=kOutput, calls=%fused_computation.30 | convolution fusion | flops 4294967296 | bytes 14680064 | tf_op jit(solution)/shard_map/dot_general | solution.py:60
  176.9 89.6 %reduce-scatter.6.cloned.1.call-done = f32[128,2048]{1,0:T(8,128)} async-done(((f32[1024,2048]{1,0:T(8,128)}), f32[128,2048]{1,0:T(8,128)}) %reduce-scatter.6.cloned.1.call-update) | async-done | bytes 1048592 | tf_op jit(solution)/shard_map/reduce_scatter | solution.py:65
  266.5 2.1 fusion
  268.7 0.3 reduce-scatter.8.cloned.1.call-start
  269.0 5.5 %copy.14 = bf16[128,8,2,1024]{3,1,2,0:T(8,128)(2,1)} copy(bf16[128,8,2,1024]{3,2,1,0:T(2,128)(2,1)} %bitcast.58) | data formatting | bytes 8388608
  274.5 39.7 %all-gather.8.cloned.1.call-done = bf16[1024,2048]{1,0:T(8,128)(2,1)} async-done(((bf16[128,2048]{1,0:T(8,128)(2,1)}), bf16[1024,2048]{1,0:T(8,128)(2,1)}) %all-gather.8.cloned.1.call-update) | async-done | bytes 4194320 | tf_op jit(solution)/shard_map/all_gather | solution.py:68
  314.2 9.9 %fusion.7 = f32[1024,1024]{1,0:T(8,128)} fusion(bf16[1024,2048]{1,0:T(8,128)(2,1)} %all-gather.8.cloned.1.call-done, bf16[1024,2048]{1,0:T(8,128)(2,1)} %bitcast.65), kind=kOutput, calls=%fused_computation.31 | convolution fusion | flops 4294967296 | bytes 12582912 | tf_op jit(solution)/shard_map/dot_general | solution.py:47
  324.1 1.2 copy-done.2
  325.3 0.1 convert_bitcast_fusion.1
  325.4 50.3 %reduce-scatter.8.cloned.1.call-done = f32[256,1024]{1,0:T(8,128)} async-done(((f32[1024,1024]{1,0:T(8,128)}), f32[256,1024]{1,0:T(8,128)}) %reduce-scatter.8.cloned.1.call-update) | async-done | bytes 1048592 | tf_op jit(solution)/shard_map/reduce_scatter | solution.py:70
  375.7 1.3 convert_bitcast_fusion
  377.0 0.1 pad_maximum_fusion
  377.1 0.1 collective-permute-start
  377.2 16.0 %collective-permute-done = bf16[256,2,1,1024]{3,0,1,2:T(8,128)(2,1)S(1)} collective-permute-done((bf16[256,2,1,1024]{3,0,1,2:T(8,128)(2,1)S(1)}, bf16[256,2,1,1024]{3,0,1,2:T(8,128)(2,1)S(1)}, u32[]{:S(2)}, u32[]{:S(2)}) %collective-permute-start) | collective-permute-done | bytes 1048608 | tf_op jit(solution)/shard_map/ppermute | solution.py:20
  393.2 3.5 collective-permute-start.4
  396.8 23.8 %collective-permute-done.1 = bf16[256,2,1,1024]{3,0,1,2:T(8,128)(2,1)} collective-permute-done((bf16[256,2,1,1024]{3,0,1,2:T(8,128)(2,1)S(1)}, bf16[256,2,1,1024]{3,0,1,2:T(8,128)(2,1)}, u32[]{:S(2)}, u32[]{:S(2)}) %collective-permute-start.1) | collective-permute-done | bytes 1048608 | tf_op jit(solution)/shard_map/ppermute | solution.py:20
  420.6 3.5 collective-permute-start.5
  424.1 22.6 %collective-permute-done.2 = bf16[256,2,1,1024]{3,0,1,2:T(8,128)(2,1)} collective-permute-done((bf16[256,2,1,1024]{3,0,1,2:T(8,128)(2,1)}, bf16[256,2,1,1024]{3,0,1,2:T(8,128)(2,1)}, u32[]{:S(2)}, u32[]{:S(2)}) %collective-permute-start.2) | collective-permute-done | bytes 1048608 | tf_op jit(solution)/shard_map/ppermute | solution.py:20
  446.8 3.6 collective-permute-start.6
  450.4 20.4 %collective-permute-done.3 = bf16[256,2,1,1024]{3,0,1,2:T(8,128)(2,1)S(1)} collective-permute-done((bf16[256,2,1,1024]{3,0,1,2:T(8,128)(2,1)}, bf16[256,2,1,1024]{3,0,1,2:T(8,128)(2,1)S(1)}, u32[]{:S(2)}, u32[]{:S(2)}) %collective-permute-start.3) | collective-permute-done | bytes 1048608 | tf_op jit(solution)/shard_map/ppermute | solution.py:20
  470.8 1.0 bitcast_dynamic-update-slice_fusion.7
  471.9 2.3 bitcast_dynamic-update-slice_fusion.6
  474.1 2.3 bitcast_dynamic-update-slice_fusion.5
  476.4 1.1 bitcast_dynamic-update-slice_fusion.4
  477.5 1.0 bitcast_dynamic-update-slice_fusion.3
  478.5 2.3 bitcast_dynamic-update-slice_fusion.2
  480.8 1.0 bitcast_dynamic-update-slice_fusion.1
  481.8 1.1 bitcast_dynamic-update-slice_fusion
  483.0 8.1 %gather_fusion = bf16[8,256,2,1024]{3,1,2,0:T(8,128)(2,1)} fusion(bf16[8,256,2,1024]{3,1,2,0:T(8,128)(2,1)} %bitcast.11, s32[1024]{0:T(1024)S(1)} %pad_clamp_fusion), kind=kCustom, calls=%fused_computation | custom fusion | bytes 16777248 | tf_op jit(solution)/shard_map/gather | solution.py:25
  491.0 11.9 %copy.8 = bf16[256,2,8,1,1024]{0,4,2,1,3:T(8,128)(2,1)} copy(bf16[256,2,8,1,1024]{4,0,1,2,3:T(8,128)(2,1)} %bitcast.56) | data formatting | bytes 16777216 | tf_op jit(solution)/shard_map/transpose | solution.py:8
  502.9 11.1 %gather_fusion.1 = bf16[2048,256]{1,0:T(8,128)(2,1)S(1)} fusion(bf16[256,16384]{0,1:T(8,128)(2,1)} %bitcast.57, s32[2048]{0:T(1024)S(1)} %broadcast_clamp_fusion), kind=kCustom, calls=%fused_computation.1 | custom fusion | bytes 2105344 | tf_op jit(solution)/shard_map/jit(_take)/gather | solution.py:75
  514.0 1.1 copy.9
  515.1 1.9 broadcast_select_fusion
  (25 shorter events, 0.2 us)
Async XLA Ops:
  6.5 60.7 %all-gather.4.cloned.1.call-start = ((), (), s32[]{:S(2)}) async-start(), calls=%async_computation.3 | async-start | bytes 4718592 | tf_op jit(solution)/shard_map/all_gather | solution.py:55
  15.3 1.3 copy-start
  17.5 111.3 %reduce-scatter.4.cloned.1.call-start = ((), (), s32[]{:S(2)}) async-start(), calls=%async_computation.4 | async-start | bytes 5242880 | tf_op jit(solution)/shard_map/reduce_scatter | solution.py:57
  77.2 89.0 %all-gather.6.cloned.1.call-start = ((), (), s32[]{:S(2)}) async-start(), calls=%async_computation.5 | async-start | bytes 2621440 | tf_op jit(solution)/shard_map/all_gather | solution.py:61
  130.9 135.6 %reduce-scatter.6.cloned.1.call-start = ((), (), s32[]{:S(2)}) async-start(), calls=%async_computation.6 | async-start | bytes 9437184 | tf_op jit(solution)/shard_map/reduce_scatter | solution.py:65
  176.8 89.7 %copy-start.1 = (f32[16,8,4,1024]{3,1,2,0:T(8,128)S(1)}, f32[16,8,4,1024]{3,1,2,0:T(8,128)}, u32[]{:S(2)}) copy-start(f32[16,8,4,1024]{3,1,2,0:T(8,128)} %copy-done) | copy-start | bytes 6291460
  176.9 137.3 %all-gather.8.cloned.1.call-start = ((), (), s32[]{:S(2)}) async-start(), calls=%async_computation.7 | async-start | bytes 4718592 | tf_op jit(solution)/shard_map/all_gather | solution.py:68
  268.7 107.0 %reduce-scatter.8.cloned.1.call-start = ((), (), s32[]{:S(2)}) async-start(), calls=%async_computation.8 | async-start | bytes 5242880 | tf_op jit(solution)/shard_map/reduce_scatter | solution.py:70
  324.1 1.2 copy-start.2
  325.3 121.4 %copy-start.3 = (s32[2,1,1024]{2,1,0:T(1,128)S(1)}, s32[2,1,1024]{2,1,0:T(1,128)}, u32[]{:S(2)}) copy-start(s32[2,1,1024]{2,1,0:T(1,128)} %param.7) | copy-start | bytes 24580
  377.1 16.1 %collective-permute-start = (bf16[256,2,1,1024]{3,0,1,2:T(8,128)(2,1)S(1)}, bf16[256,2,1,1024]{3,0,1,2:T(8,128)(2,1)S(1)}, u32[]{:S(2)}, u32[]{:S(2)}) collective-permute-start(bf16[256,2,1,1024]{3,0,1,2:T(8,128)(2,1)S(1)} %get-tuple-element.8), channel_id=1, source_target_pairs={{0,4},{4,8},{8,12},{12,16},{16,20},{20,24},{24,28},{28,0},{1,5},{5... | collective-permute-start | bytes 3145736 | tf_op jit(solution)/shard_map/ppermute | solution.py:20
  393.2 27.3 %collective-permute-start.1 = (bf16[256,2,1,1024]{3,0,1,2:T(8,128)(2,1)S(1)}, bf16[256,2,1,1024]{3,0,1,2:T(8,128)(2,1)}, u32[]{:S(2)}, u32[]{:S(2)}) collective-permute-start(bf16[256,2,1,1024]{3,0,1,2:T(8,128)(2,1)S(1)} %collective-permute-done), channel_id=1, source_target_pairs={{0,4},{4,8},{8,12},{12,16},{16,20},{20,24},{24,28},{28,0},{1,5},{5... | collective-permute-start | bytes 3145736 | tf_op jit(solution)/shard_map/ppermute | solution.py:20
  393.2 27.3 %collective-permute-start.4 = (bf16[256,2,1,1024]{3,0,2,1:T(8,128)(2,1)S(1)}, bf16[256,2,1,1024]{3,0,2,1:T(8,128)(2,1)}, u32[]{:S(2)}, u32[]{:S(2)}) collective-permute-start(bf16[256,2,1,1024]{3,0,2,1:T(8,128)(2,1)S(1)} %get-tuple-element.7), channel_id=1, source_target_pairs={{4,0},{8,4},{12,8},{16,12},{20,16},{24,20},{28,24},{0,28},{5,1},{9... | collective-permute-start | bytes 3145736 | tf_op jit(solution)/shard_map/ppermute | solution.py:22
  420.6 26.2 %collective-permute-start.2 = (bf16[256,2,1,1024]{3,0,1,2:T(8,128)(2,1)}, bf16[256,2,1,1024]{3,0,1,2:T(8,128)(2,1)}, u32[]{:S(2)}, u32[]{:S(2)}) collective-permute-start(bf16[256,2,1,1024]{3,0,1,2:T(8,128)(2,1)} %collective-permute-done.1), channel_id=1, source_target_pairs={{0,4},{4,8},{8,12},{12,16},{16,20},{20,24},{24,28},{28,0},{1,5},{5... | collective-permute-start | bytes 3145736 | tf_op jit(solution)/shard_map/ppermute | solution.py:20
  420.6 26.3 %collective-permute-start.5 = (bf16[256,2,1,1024]{3,0,2,1:T(8,128)(2,1)}, bf16[256,2,1,1024]{3,0,2,1:T(8,128)(2,1)S(1)}, u32[]{:S(2)}, u32[]{:S(2)}) collective-permute-start(bf16[256,2,1,1024]{3,0,2,1:T(8,128)(2,1)} %collective-permute-done.4), channel_id=1, source_target_pairs={{4,0},{8,4},{12,8},{16,12},{20,16},{24,20},{28,24},{0,28},{5,1},{9... | collective-permute-start | bytes 3145736 | tf_op jit(solution)/shard_map/ppermute | solution.py:22
  446.7 24.1 %collective-permute-start.3 = (bf16[256,2,1,1024]{3,0,1,2:T(8,128)(2,1)}, bf16[256,2,1,1024]{3,0,1,2:T(8,128)(2,1)S(1)}, u32[]{:S(2)}, u32[]{:S(2)}) collective-permute-start(bf16[256,2,1,1024]{3,0,1,2:T(8,128)(2,1)} %collective-permute-done.2), channel_id=1, source_target_pairs={{0,4},{4,8},{8,12},{12,16},{16,20},{20,24},{24,28},{28,0},{1,5},{5... | collective-permute-start | bytes 3145736 | tf_op jit(solution)/shard_map/ppermute | solution.py:20
  446.8 35.0 %collective-permute-start.6 = (bf16[256,2,1,1024]{3,0,2,1:T(8,128)(2,1)S(1)}, bf16[256,2,1,1024]{3,0,2,1:T(8,128)(2,1)S(1)}, u32[]{:S(2)}, u32[]{:S(2)}) collective-permute-start(bf16[256,2,1,1024]{3,0,2,1:T(8,128)(2,1)S(1)} %collective-permute-done.5), channel_id=1, source_target_pairs={{4,0},{8,4},{12,8},{16,12},{20,16},{24,20},{28,24},{0,28},{5,1},{9... | collective-permute-start | bytes 3145736 | tf_op jit(solution)/shard_map/ppermute | solution.py:22
Sparse Core Ops, SparseCore 0:
  17.6 49.5 all-gather.3
  77.4 51.3 reduce-scatter.3
  131.0 35.1 all-gather.5
  177.0 89.5 reduce-scatter.5
  268.8 45.3 all-gather.7
  324.2 51.3 reduce-scatter.7
